TPU v7x, 512 devices: a whole 4x8x8 slice. The times are simulated.
512 devices in a mesh: row: 16 (over y, x_lo), col: 16 (over z, x_hi), depth: 2 (over core).
Axes of the slice: x: 4 (x_hi: 2, x_lo: 2; x = x_hi * 2 + x_lo), y: 8, z: 8, core: 2. Of those that a mesh axis runs over, the one named last changes fastest.
Arguments:
- grad_out: bfloat16 [4096, 8192], P('col', 'row'), may hold values from -6 to 6
- hidden: bfloat16 [4096, 14336], P('row', 'col'), may hold values from -0.25 to 0.25
- weight: bfloat16 [8192, 14336], P('row', 'col'), may hold values from -0.046875 to 0.046875
Outputs:
- grad_hidden: bfloat16 [4096, 14336], P('row', 'col')
- grad_weight: bfloat16 [8192, 14336], P('row', 'col')
All inputs are finite; a program needn't handle non-finite values.
Results may differ from a plain program's by a relative error of at most 0.0034.
Values may be sent and summed in bfloat16 or wider, within the bound.
A program may use at most 64 MiB of HBM per device.

v0:
```python
import jax
import jax.numpy as jnp
from jax import lax
from jax.sharding import Mesh
from jax.sharding import PartitionSpec as P

ROW = ("row_0", "row_1")


def own_rows(total, axes):
    for axis in axes:
        total = lax.psum_scatter(total, axis, scatter_dimension=0, tiled=True)
    return total


def turned_gather(arrays, axis, dims):
    turned = [jnp.moveaxis(a, dim, 0) for a, dim in zip(arrays, dims)]
    both = jnp.concatenate([t.reshape(len(t), -1) for t in turned], axis=1)
    filled, at, outs = (lax.all_gather(both, axis, axis=0, tiled=True), 0, [])
    for t, dim in zip(turned, dims):
        slab = filled[:, at : at + t[0].size].reshape(-1, *t.shape[1:])
        outs.append(jnp.moveaxis(slab, 0, dim))
        at += t[0].size
    return tuple(outs)


def token_product(left, right):
    return lax.dot_general(
        left, right, (((0,), (0,)), ((), ())), preferred_element_type=jnp.float32
    )


def body(grad_out, hidden, weight):
    layer_count = lax.axis_size("depth")
    depth_index = lax.axis_index("depth")
    hidden_units = weight.shape[1]
    half_units = hidden_units // layer_count
    unit_start = depth_index * half_units
    own_hidden = lax.dynamic_slice_in_dim(hidden, unit_start, half_units, 1)
    own_weight = lax.dynamic_slice_in_dim(weight, unit_start, half_units, 1)
    all_grad = lax.all_gather(grad_out, "col", axis=0, tiled=True)
    all_hidden = lax.all_gather(own_hidden, ROW, axis=0, tiled=True)
    weight_half = token_product(all_grad, all_hidden).astype(jnp.bfloat16)
    hidden_half = own_rows(
        jnp.dot(all_grad, own_weight, preferred_element_type=jnp.float32), ROW
    ).astype(jnp.bfloat16)
    hidden_total, weight_total = turned_gather((hidden_half, weight_half), "depth", (1, 1))
    return (hidden_total, weight_total)


def solution(mesh):
    torus = Mesh(
        mesh.devices.reshape(8, 2, mesh.shape["col"], mesh.shape["depth"]),
        ("row_0", "row_1", "col", "depth"),
    )
    placed = (P("col", ROW), P(ROW, "col"), P(ROW, "col"))
    return jax.shard_map(
        body, mesh=torus, in_specs=placed, out_specs=(P(ROW, "col"), P(ROW, "col")), check_vma=False
    )
```

profile of v0, /device:TPU:1, one launch (start us, length us, event | category | flops | bytes accessed | tf_op | source)
XLA Modules:
  0.0 325.7 jit_solution(11276576108216204795)
XLA Ops:
  8.0 0.0 copy-start
  8.0 0.0 all-gather.4.cloned.1.call-start
  8.1 0.7 all-gather.4.cloned.1.call-update
  8.7 0.0 reduce-scatter.3.cloned.1.call-start
  8.8 111.5 %all-gather.4.cloned.1.call-done = bf16[4096,512]{1,0:T(8,128)(2,1)} async-done(((bf16[256,512]{1,0:T(8,128)(2,1)}), bf16[4096,512]{1,0:T(8,128)(2,1)}) %all-gather.4.cloned.1.call-update) | async-done | bytes 4194320 | tf_op jit(solution)/shard_map/all_gather | solution.py:41
  120.3 0.0 copy-done
  120.3 7.8 %convolution_bitcast_fusion = f32[4096,448]{0,1:T(8,128)} fusion(bf16[4096,512]{1,0:T(8,128)(2,1)} %all-gather.4.cloned.1.call-done, bf16[512,896]{1,0:T(8,128)(2,1)S(1)} %copy-done, s32[]{:T(128)S(6)} %select_n.4), kind=kOutput, calls=%fused_computation | convolution fusion | flops 1879048192 | bytes 12058628 | tf_op jit(solution)/shard_map/dot_general | solution.py:45
  128.0 0.0 copy-start.1
  128.0 0.0 reduce-scatter.3.cloned.1.call-update
  128.0 0.0 all-gather.6.cloned.1.call-start
  128.1 0.9 copy-done.1
  129.0 0.8 constant_dynamic-slice_fusion
  129.9 0.0 all-gather.6.cloned.1.call-update
  129.9 0.0 reduce-scatter.5.cloned.1.call-start
  130.0 105.5 %reduce-scatter.3.cloned.1.call-done = f32[512,448]{0,1:T(8,128)} async-done(((f32[4096,448]{0,1:T(8,128)}), f32[512,448]{0,1:T(8,128)}) %reduce-scatter.3.cloned.1.call-update) | async-done | bytes 917520 | tf_op jit(solution)/shard_map/reduce_scatter | solution.py:12
  235.5 0.0 reduce-scatter.5.cloned.1.call-update
  235.5 0.0 all-gather.8.cloned.1.call-start
  235.6 48.3 %all-gather.6.cloned.1.call-done = bf16[4096,448]{1,0:T(8,128)(2,1)} async-done(((bf16[256,448]{1,0:T(8,128)(2,1)}), bf16[4096,448]{1,0:T(8,128)(2,1)}) %all-gather.6.cloned.1.call-update) | async-done | bytes 3670032 | tf_op jit(solution)/shard_map/all_gather | solution.py:42
  283.9 5.5 %convolution_convert_fusion = bf16[448,512]{1,0:T(8,128)(2,1)S(1)} fusion(bf16[4096,448]{1,0:T(8,128)(2,1)} %all-gather.6.cloned.1.call-done, bf16[4096,512]{1,0:T(8,128)(2,1)} %all-gather.4.cloned.1.call-done), kind=kOutput, calls=%fused_computation.1 | convolution fusion | flops 1879277568 | bytes 8323072 | tf_op jit(solution)/shard_map/dot_general | solution.py:28
  289.5 0.0 reduce-scatter.5.cloned.1.call-done
  289.5 1.0 convert_bitcast_fusion
  290.5 0.9 pad_maximum_fusion
  291.4 0.0 all-gather.8.cloned.1.call-update
  291.5 22.6 %all-gather.8.cloned.1.call-done = bf16[896,768]{1,0:T(8,128)(2,1)} async-done(((bf16[448,768]{1,0:T(8,128)(2,1)}), bf16[896,768]{1,0:T(8,128)(2,1)}) %all-gather.8.cloned.1.call-update) | async-done | bytes 1376272 | tf_op jit(solution)/shard_map/all_gather | solution.py:19
  314.1 1.2 slice_bitcast_fusion
  315.3 1.3 copy.6
  316.6 1.0 slice_bitcast_fusion.1
  317.6 1.0 copy.5
Async XLA Ops:
  8.0 112.3 %copy-start = (bf16[512,896]{1,0:T(8,128)(2,1)S(1)}, bf16[512,896]{1,0:T(8,128)(2,1)}, u32[]{:S(2)}) copy-start(bf16[512,896]{1,0:T(8,128)(2,1)} %param.5) | copy-start | bytes 2752516
  8.0 112.2 %all-gather.4.cloned.1.call-start = ((), (), s32[]{:S(2)}) async-start(), calls=%async_computation.2 | async-start | bytes 4456448 | tf_op jit(solution)/shard_map/all_gather | solution.py:41
  8.7 226.7 %reduce-scatter.3.cloned.1.call-start = ((), (), s32[]{:S(2)}) async-start(), calls=%async_computation.3 | async-start | bytes 8257536 | tf_op jit(solution)/shard_map/reduce_scatter | solution.py:12
  128.0 1.0 copy-start.1
  128.0 155.9 %all-gather.6.cloned.1.call-start = ((), (), s32[]{:S(2)}) async-start(), calls=%async_computation.5 | async-start | bytes 4456448 | tf_op jit(solution)/shard_map/all_gather | solution.py:42
  129.9 159.6 %reduce-scatter.5.cloned.1.call-start = ((), (), s32[]{:S(2)}) async-start(), calls=%async_computation.4 | async-start | bytes 1376256 | tf_op jit(solution)/shard_map/reduce_scatter | solution.py:12
  235.5 78.6 %all-gather.8.cloned.1.call-start = ((), (), s32[]{:S(2)}) async-start(), calls=%async_computation.6 | async-start | bytes 2064384 | tf_op jit(solution)/shard_map/all_gather | solution.py:19
Sparse Core Ops, SparseCore 0:
  12.0 108.2 all-gather.3
  128.2 107.2 reduce-scatter.2
  238.3 30.6 reduce-scatter.4
Sparse Core Ops, SparseCore 1:
  131.2 152.7 all-gather.5
  291.5 22.5 all-gather.7
where the time goes:
time: 326 us
  waiting for transfers between devices  289 us (89%)
  between operations  15.2 us (5%)
  matrix products  13.3 us (4%)
  local copies, waits for them, and re-layouts  6.34 us (2%)
    all_gather x1, waiting for transfers between devices, body(): all_grad = lax.all_gather(grad_out, 'col', axis=0, tiled=True)  111 us
    reduce_scatter x2, waiting for transfers between devices, own_rows(): total = lax.psum_scatter(total, axis, scatter_dimension=0, tiled=True)  106 us
    all_gather x1, waiting for transfers between devices, body(): all_hidden = lax.all_gather(own_hidden, ROW, axis=0, tiled=True)  48.3 us
    all_gather x1, waiting for transfers between devices, turned_gather(): filled, at, outs = (lax.all_gather(both, axis, axis=0, tiled=True), 0, [])  22.6 us
    dot_general x1, matrix products, body(): jnp.dot(all_grad, own_weight, preferred_element_type=jnp.float32)  7.76 us
  transfers between devices with their start and end apart: 5, of which 4 were waited for; matrix products, arithmetic and copies ran while one was open for 2% of the time, Pallas kernels for 0%

commit v1 on v0

v1 whole, which is shorter than its diff:
```python
import jax
import jax.numpy as jnp
from jax import lax
from jax.experimental import pallas as pl
from jax.experimental.pallas import tpu as pltpu
from jax.sharding import PartitionSpec as P

MESH = pl.DeviceIdType.MESH
BF16, F32 = jnp.bfloat16, jnp.float32
RING = 8
HOPS = [
    (sign, other, hop)
    for hop in (1, 2, 3, 4)
    for other in (0, 1)
    for sign in (1, -1)
    if hop < 4 or (sign == 1) == (other == 0)
]


def wrap(pos):
    return lax.rem(pos + RING, RING)


class Gather:
    def __init__(self, axis, own, full, send, recv):
        at = lax.axis_index(axis)
        self.axis, self.own, self.full, self.send, self.recv = axis, own, full, send, recv
        self.pos, self.lane = at // 2, lax.rem(at, 2)

    def device(self, pos, lane):
        return {self.axis: wrap(pos) * 2 + lane}

    def slot(self, pos, lane):
        return wrap(pos) * 2 + lane

    def copy(self, src, slot, key, device):
        return pltpu.make_async_remote_copy(
            src_ref=src,
            dst_ref=self.full.at[slot],
            send_sem=self.send.at[key],
            recv_sem=self.recv.at[key],
            device_id=device,
            device_id_type=MESH,
        )

    def swap(self):
        slot = self.slot(self.pos, self.lane)
        return self.copy(self.own, slot, len(HOPS), self.device(self.pos, 1 - self.lane))

    def swapped(self):
        slot = self.slot(self.pos, 1 - self.lane)
        device = self.device(self.pos, 1 - self.lane)
        self.copy(self.full.at[slot], slot, len(HOPS), device).wait_recv()

    def hop(self, sign, other, hop):
        lane = 1 - self.lane if other else self.lane
        slot = self.slot(self.pos - sign * (hop - 1), lane)
        src = self.own if hop == 1 and not other else self.full.at[slot]
        key = HOPS.index((sign, other, hop))
        return self.copy(src, slot, key, self.device(self.pos + sign, self.lane))

    def arrived(self, sign, other, hop):
        lane = 1 - self.lane if other else self.lane
        slot = self.slot(self.pos - sign * hop, lane)
        key = HOPS.index((sign, other, hop))
        device = self.device(self.pos - sign, self.lane)
        self.copy(self.full.at[slot], slot, key, device).wait_recv()

    def round(self, hop, sent):
        for sign, other, step in HOPS:
            if step == hop:
                self.arrived(sign, other, hop)
                if (sign, other, hop + 1) in HOPS:
                    sent.append(self.hop(sign, other, hop + 1))
                    sent[-1].start()


def kernel(
    g_ref, h_ref, w_ref, gh_ref, gw_ref,
    ga, ha, kept, xs, xr, ys, yr, acc, acc_in, half_s, half_r,
    g_send, g_recv, h_send, h_recv, x_send, x_recv, y_send, y_recv, d_send, d_recv,
):
    depth = lax.axis_index("depth")
    half = g_ref.shape[0] // 2
    quarter = half // 2
    mine = pl.ds(pl.multiple_of(depth * half, half), half)
    gathers = (
        Gather("col", g_ref.at[mine], ga, g_send, g_recv),
        Gather("row", h_ref.at[mine], ha, h_send, h_recv),
    )
    grad, hidden = gathers
    y, lane = hidden.pos, hidden.lane

    def row_device(pos):
        return {"row": wrap(pos) * 2 + lane}

    partner = {"row": y * 2 + 1 - lane}
    sibling = {"depth": 1 - depth}

    barrier = pltpu.get_barrier_semaphore()
    peers = [partner, sibling, grad.device(grad.pos, 1 - grad.lane)]
    peers += [grad.device(grad.pos + k, grad.lane) for k in (-1, 1)]
    peers += [row_device(y + k) for k in (-3, -2, -1, 1, 2, 3)]
    for peer in peers:
        pl.semaphore_signal(barrier, inc=1, device_id=peer, device_id_type=MESH)
    pl.semaphore_wait(barrier, len(peers))

    sent = []

    def start(copy):
        copy.start()
        sent.append(copy)

    for gather in gathers:
        start(gather.swap())
        for sign in (1, -1):
            start(gather.hop(sign, 0, 1))
    for gather in gathers:
        gather.full[gather.slot(gather.pos, gather.lane)] = gather.own[...]

    def across(pos, at):
        pos = wrap(pos)
        return pltpu.make_async_remote_copy(
            src_ref=xs.at[pos],
            dst_ref=xr.at[pos],
            send_sem=x_send.at[at],
            recv_sem=x_recv.at[at],
            device_id=partner,
            device_id_type=MESH,
        )

    def product(pos, at):
        pos = wrap(pos)
        away = jnp.dot(ga[pos * 2 + 1 - lane], w_ref[...], preferred_element_type=F32)
        xs[pos] = away.astype(BF16)
        start(across(pos, at))
        kept[pos] = jnp.dot(ga[pos * 2 + lane], w_ref[...], preferred_element_type=F32)

    def products(hop):
        product(grad.pos - hop, 2 * hop - 1)
        if hop < 4:
            product(grad.pos + hop, 2 * hop)

    def second_lane(gather):
        gather.swapped()
        for sign in (1, -1):
            start(gather.hop(sign, 1, 1))

    second_lane(grad)
    product(grad.pos, 0)
    second_lane(hidden)
    grad.round(1, sent)
    products(1)
    hidden.round(1, sent)
    grad.round(2, sent)
    products(2)
    grad.round(3, sent)
    products(3)
    hidden.round(2, sent)
    grad.round(4, sent)
    products(4)
    hidden.round(3, sent)

    for hop in range(5):
        across(grad.pos - hop, max(2 * hop - 1, 0)).wait_recv()
        if 0 < hop < 4:
            across(grad.pos + hop, 2 * hop).wait_recv()

    def total(pos, rows):
        pos = wrap(pos)
        return kept[pos, rows] + xr[pos, rows].astype(F32)

    plans, at = [], 0
    for sign in (1, -1):
        for part in (0, 1):
            far = 4 if (part == 0) == (sign == 1) else 3
            plans.append((sign, pl.ds(part * quarter, quarter), far, at, part))
            at += far

    def along(key, pos):
        return pltpu.make_async_remote_copy(
            src_ref=ys.at[key],
            dst_ref=yr.at[key],
            send_sem=y_send.at[key],
            recv_sem=y_recv.at[key],
            device_id=row_device(pos),
            device_id_type=MESH,
        )

    def emit(key, value, pos):
        ys[key] = value.astype(BF16)
        start(along(key, pos))

    for sign, rows, far, key, _ in plans:
        emit(key, total(y + sign * far, rows), y + sign)
    for sign, rows, far, key, _ in plans:
        if far == 4:
            emit(key + 2, total(y + sign * 2, rows), y + sign)
    for sign, rows, far, key, _ in plans:
        if far == 3:
            emit(key + 2, total(y + sign, rows), y + sign)

    hidden.round(4, sent)

    for sign, rows, far, key, _ in plans:
        along(key, y).wait_recv()
        value = total(y + sign * (far - 1), rows) + yr[key].astype(F32)
        emit(key + 1, value, y + sign * (far - 1))
    for sign, rows, far, key, _ in plans:
        if far == 4:
            along(key + 2, y).wait_recv()
            value = total(y + sign, rows) + yr[key + 2].astype(F32)
            emit(key + 3, value, y + sign)

    acc[...] = jnp.zeros_like(acc)
    chunk = 4

    @pl.loop(0, 2 * RING // chunk)
    def _(step):
        tokens = pl.ds(step * chunk, chunk)
        left = ga[tokens].reshape(chunk * half, -1)
        right = ha[tokens].reshape(chunk * half, -1)
        acc[...] += lax.dot_general(
            left, right, (((0,), (0,)), ((), ())), preferred_element_type=F32
        )

    def to_sibling(src, dst, key):
        return pltpu.make_async_remote_copy(
            src_ref=src,
            dst_ref=dst,
            send_sem=d_send.at[key],
            recv_sem=d_recv.at[key],
            device_id=sibling,
            device_id_type=MESH,
        )

    weight_swap = to_sibling(acc, acc_in, 0)
    start(weight_swap)
    weight_swap.wait_recv()
    gw_ref[...] = (acc[...] + acc_in[...]).astype(BF16)

    for part in (0, 1):
        rows = pl.ds(part * quarter, quarter)
        value = total(y, rows)
        for sign, _, far, key, which in plans:
            if which == part:
                for last in (key + 1, key + 3 if far == 4 else key + 2):
                    along(last, y).wait_recv()
                    value += yr[last].astype(F32)
        half_s[rows] = value.astype(BF16)
    half_swap = to_sibling(half_s, half_r, 1)
    start(half_swap)
    gh_ref[mine] = half_s[...]
    half_swap.wait_recv()
    gh_ref[pl.ds(pl.multiple_of((1 - depth) * half, half), half)] = half_r[...]
    for copy in sent:
        copy.wait_send()


def body(grad_out, hidden, weight):
    (tokens, features), units = grad_out.shape, hidden.shape[1]
    half, quarter, blocks = tokens // 2, tokens // 4, 2 * RING
    dma = pltpu.SemaphoreType.DMA
    vmem = pl.BlockSpec(memory_space=pltpu.VMEM)
    swaps = len(HOPS) + 1
    return pl.pallas_call(
        kernel,
        out_shape=(
            jax.ShapeDtypeStruct(hidden.shape, BF16),
            jax.ShapeDtypeStruct(weight.shape, BF16),
        ),
        in_specs=[vmem] * 3,
        out_specs=(vmem, vmem),
        scratch_shapes=[
            pltpu.VMEM((blocks, half, features), BF16),
            pltpu.VMEM((blocks, half, units), BF16),
            pltpu.VMEM((RING, half, units), F32),
            pltpu.VMEM((RING, half, units), BF16),
            pltpu.VMEM((RING, half, units), BF16),
            pltpu.VMEM((14, quarter, units), BF16),
            pltpu.VMEM((14, quarter, units), BF16),
            pltpu.VMEM((features, units), F32),
            pltpu.VMEM((features, units), F32),
            pltpu.VMEM((half, units), BF16),
            pltpu.VMEM((half, units), BF16),
            dma((swaps,)), dma((swaps,)), dma((swaps,)), dma((swaps,)),
            dma((RING,)), dma((RING,)), dma((14,)), dma((14,)), dma((2,)), dma((2,)),
        ],
        compiler_params=pltpu.CompilerParams(
            collective_id=0, has_side_effects=True, vmem_limit_bytes=56 << 20
        ),
    )(grad_out, hidden, weight)


def solution(mesh):
    return jax.shard_map(
        body,
        mesh=mesh,
        in_specs=(P("col", "row"), P("row", "col"), P("row", "col")),
        out_specs=(P("row", "col"), P("row", "col")),
        check_vma=False,
    )
```

time: 326 us -> 95.6 us (0.29)
  waiting for transfers between devices: 289 us -> 0 us
  Pallas kernels: 0 us -> 92 us
  between operations: 15.2 us -> 0.65 us
  matrix products: 13.3 us -> 0 us
  local copies, waits for them, and re-layouts: 6.34 us -> 2.83 us
    all_gather x3 -> x0, waiting for transfers between devices: 182 us -> none  [the longest x1 111 us: body(): all_grad = lax.all_gather(grad_out, 'col', axis=0, tiled=True)]
    reduce_scatter x2 -> x0, waiting for transfers between devices: 106 us -> none  [own_rows(): total = lax.psum_scatter(total, axis, scatter_dimension=0, tiled=True)]
    pallas_call x0 -> x1, Pallas kernels: none -> 92 us  [body(): pl.pallas_call(kernel, out_shape=(jax.ShapeDtypeStruct(hidden.shape, BF16...]
    dot_general x2 -> x0, matrix products: 13.3 us -> none  [the longest x1 7.76 us: body(): jnp.dot(all_grad, own_weight, preferred_element_type=jnp.float32)]
  transfers between devices with their start and end apart: 5 -> 0, of which waited for: 4 -> 0; matrix products, arithmetic and copies ran while one was open for 2% -> 0% of each run, Pallas kernels for 0% -> 0%
where the time goes in v1:
time: 95.6 us; the launch traced here: 95.5 us
  Pallas kernels  92 us (96%)
  local copies, waits for them, and re-layouts  2.83 us (3%)
    pallas_call x1, Pallas kernels, body(): pl.pallas_call(kernel, out_shape=(jax.ShapeDtypeStruct(hidden.shape, BF16...  92 us
    unnamed x4, local copies, waits for them, and re-layouts  2.83 us

profile of v1, /device:TPU:1, one launch (start us, length us, event | category | flops | bytes accessed | tf_op | source)
XLA Modules:
  0.0 95.5 jit_solution(8429440825215411357)
XLA Ops:
  0.6 92.0 %shard_map.50 = (bf16[256,896]{1,0:T(8,128)(2,1)}, bf16[512,896]{1,0:T(8,128)(2,1)}) custom-call(bf16[256,512]{1,0:T(8,128)(2,1)} %g_ref.1, bf16[256,896]{1,0:T(8,128)(2,1)} %h_ref.1, bf16[512,896]{1,0:T(8,128)(2,1)} %w_ref.1), custom_call_target="tpu_custom_call" | custom-call | tf_op jit(solution)/shard_map/pallas_call | solution.py:266
  92.6 0.0 copy-start
  92.6 1.9 %copy.7 = bf16[256,896]{1,0:T(8,128)(2,1)} copy(bf16[256,896]{1,0:T(8,128)(2,1)} %get-tuple-element.4) | data formatting | bytes 917504
  94.5 0.0 copy-done
  94.5 0.9 copy.8
Async XLA Ops:
  92.6 1.9 %copy-start = (bf16[512,896]{1,0:T(8,128)(2,1)S(1)}, bf16[512,896]{1,0:T(8,128)(2,1)}, u32[]{:S(2)}) copy-start(bf16[512,896]{1,0:T(8,128)(2,1)} %get-tuple-element.5) | copy-start | bytes 2752516

commit v2 on v1

v2 whole, which is shorter than its diff:
```python
import jax
import jax.numpy as jnp
from jax import lax
from jax.experimental import pallas as pl
from jax.experimental.pallas import tpu as pltpu
from jax.sharding import PartitionSpec as P

MESH = pl.DeviceIdType.MESH
BF16, F32 = jnp.bfloat16, jnp.float32
RING = 8
GRAD_HOPS = [
    (sign, lane, hop)
    for hop in (1, 2, 3, 4)
    for lane in (0, 1, 2)
    for sign in (1, -1)
    if hop < 4 or (sign == 1) == (lane != 1)
]
HIDDEN_HOPS = [(1, 0, 1), (-1, 0, 1), (1, 0, 2), (-1, 0, 2), (1, 0, 3), (-1, 0, 3), (1, 0, 4)]
HIDDEN_HOPS += [(1, 1, 1), (-1, 1, 1), (-1, 1, 2)]
HANDED = [(1, 0, 2), (1, 0, 3), (-1, 0, 3), (1, 0, 4)]


def wrap(pos):
    return lax.rem(pos + RING, RING)


class Gather:
    def __init__(self, axis, hops, own, full, send, recv):
        at = lax.axis_index(axis)
        self.axis, self.hops, self.own, self.full = axis, hops, own, full
        self.send, self.recv = send, recv
        self.pos, self.lane = at // 2, lax.rem(at, 2)

    def device(self, pos, lane):
        return {self.axis: wrap(pos) * 2 + lane}

    def slot(self, pos, lane):
        if lane == 2:
            return 2 * RING + wrap(pos)
        return wrap(pos) * 2 + (1 - self.lane if lane else self.lane)

    def copy(self, src, slot, key, device):
        return pltpu.make_async_remote_copy(
            src_ref=src,
            dst_ref=self.full.at[slot],
            send_sem=self.send.at[key],
            recv_sem=self.recv.at[key],
            device_id=device,
            device_id_type=MESH,
        )

    def partner(self):
        return self.device(self.pos, 1 - self.lane)

    def swap(self):
        return self.copy(self.own, self.slot(self.pos, 0), len(self.hops), self.partner())

    def swapped(self):
        slot = self.slot(self.pos, 1)
        self.copy(self.full.at[slot], slot, len(self.hops), self.partner()).wait_recv()

    def hop(self, sign, lane, hop):
        slot = self.slot(self.pos - sign * (hop - 1), lane)
        src = self.own if hop == 1 and not lane else self.full.at[slot]
        key = self.hops.index((sign, lane, hop))
        return self.copy(src, slot, key, self.device(self.pos + sign, self.lane))

    def arrived(self, sign, lane, hop):
        slot = self.slot(self.pos - sign * hop, lane)
        key = self.hops.index((sign, lane, hop))
        device = self.device(self.pos - sign, self.lane)
        self.copy(self.full.at[slot], slot, key, device).wait_recv()

    def hand(self, index):
        sign, _, hop = HANDED[index]
        slot = self.slot(self.pos - sign * hop, 0)
        return self.copy(self.full.at[slot], slot, len(self.hops) + 1 + index, self.partner())

    def handed(self, index):
        sign, _, hop = HANDED[index]
        slot = self.slot(self.pos - sign * hop, 1)
        key = len(self.hops) + 1 + index
        self.copy(self.full.at[slot], slot, key, self.partner()).wait_recv()


def kernel(
    g_ref, h_ref, w_ref, gh_ref, gw_ref,
    ga, ha, wo, kept, ys, yr, acc, acc_in, half_s, half_r,
    g_send, g_recv, h_send, h_recv, w_send, w_recv, y_send, y_recv, d_send, d_recv,
):
    depth = lax.axis_index("depth")
    half = g_ref.shape[0] // 2
    quarter = half // 2
    mine = pl.ds(pl.multiple_of(depth * half, half), half)
    grad = Gather("col", GRAD_HOPS, g_ref.at[mine], ga, g_send, g_recv)
    hidden = Gather("row", HIDDEN_HOPS, h_ref.at[mine], ha, h_send, h_recv)
    y, lane = hidden.pos, hidden.lane

    def row_device(pos):
        return {"row": wrap(pos) * 2 + lane}

    partner = hidden.partner()
    sibling = {"depth": 1 - depth}
    across = partner | grad.partner()

    barrier = pltpu.get_barrier_semaphore()
    peers = [partner, sibling, across, grad.partner()]
    peers += [grad.device(grad.pos + k, grad.lane) for k in (-1, 1)]
    peers += [row_device(y + k) for k in (-3, -2, -1, 1, 2, 3)]
    for peer in peers:
        pl.semaphore_signal(barrier, inc=1, device_id=peer, device_id_type=MESH)
    pl.semaphore_wait(barrier, len(peers))

    sent = []

    def start(copy):
        copy.start()
        sent.append(copy)

    lane_2 = len(GRAD_HOPS) + 1
    third = [grad.copy(grad.own, grad.slot(grad.pos, 2), lane_2 + i, to) for i, to in enumerate((partner, across))]

    def third_arrived():
        slot = grad.slot(grad.pos, 2)
        for i, (source, here) in enumerate(((partner, lane == grad.lane), (across, lane != grad.lane))):
            @pl.when(here)
            def _():
                grad.copy(ga.at[slot], slot, lane_2 + i, source).wait_recv()

    features = w_ref.shape[0] // 2
    part = pl.ds(pl.multiple_of(depth * features, features), features)
    rest = pl.ds(pl.multiple_of((1 - depth) * features, features), features)

    def weights(src, rows, key, device):
        return pltpu.make_async_remote_copy(
            src_ref=src.at[rows],
            dst_ref=wo.at[rows],
            send_sem=w_send.at[key],
            recv_sem=w_recv.at[key],
            device_id=device,
            device_id_type=MESH,
        )

    for sign in (1, -1):
        start(grad.hop(sign, 0, 1))
    @pl.when(lane != grad.lane)
    def _():
        for copy in third:
            copy.start()
    start(grad.swap())
    for sign in (1, -1):
        start(hidden.hop(sign, 0, 1))
    start(weights(w_ref, part, 0, partner))
    start(hidden.swap())
    for gather in (grad, hidden):
        gather.full[gather.slot(gather.pos, 0)] = gather.own[...]

    def grad_round(hop):
        for key in GRAD_HOPS:
            if key[2] == hop:
                grad.arrived(*key)
                following = (*key[:2], hop + 1)
                if following in GRAD_HOPS:
                    start(grad.hop(*following))

    def hidden_round(lane, hop):
        for key in HIDDEN_HOPS:
            if key[1:] == (lane, hop):
                hidden.arrived(*key)
                following = (*key[:2], hop + 1)
                if following in HIDDEN_HOPS:
                    start(hidden.hop(*following))
                if key in HANDED:
                    start(hidden.hand(HANDED.index(key)))

    def product(pos):
        pos = wrap(pos)
        value = jnp.dot(ga[pos * 2 + lane], w_ref[...], preferred_element_type=F32)
        kept[pos] = value + jnp.dot(ga[2 * RING + pos], wo[...], preferred_element_type=F32)

    def products(hop):
        product(grad.pos - hop)
        if hop < 4:
            product(grad.pos + hop)

    third_arrived()
    for sign in (1, -1):
        start(grad.hop(sign, 2, 1))
    grad.swapped()
    for sign in (1, -1):
        start(grad.hop(sign, 1, 1))
    hidden_round(0, 1)
    grad_round(1)
    weights(w_ref, part, 0, partner).wait_recv()
    start(weights(wo, part, 1, sibling))
    hidden_round(0, 2)
    hidden.swapped()
    for sign in (1, -1):
        start(hidden.hop(sign, 1, 1))
    weights(wo, rest, 1, sibling).wait_recv()
    product(grad.pos)
    products(1)
    grad_round(2)
    hidden_round(0, 3)
    products(2)
    hidden_round(1, 1)
    grad_round(3)
    products(3)
    hidden_round(0, 4)
    grad_round(4)
    products(4)

    def total(pos, rows):
        return kept[wrap(pos), rows]

    plans, at = [], 0
    for sign in (1, -1):
        for part in (0, 1):
            far = 4 if (part == 0) == (sign == 1) else 3
            plans.append((sign, pl.ds(part * quarter, quarter), far, at, part))
            at += far

    def along(key, pos):
        return pltpu.make_async_remote_copy(
            src_ref=ys.at[key],
            dst_ref=yr.at[key],
            send_sem=y_send.at[key],
            recv_sem=y_recv.at[key],
            device_id=row_device(pos),
            device_id_type=MESH,
        )

    def emit(key, value, pos):
        ys[key] = value.astype(BF16)
        start(along(key, pos))

    for sign, rows, far, key, _ in plans:
        emit(key, total(y + sign * far, rows), y + sign)
    for sign, rows, far, key, _ in plans:
        if far == 4:
            emit(key + 2, total(y + sign * 2, rows), y + sign)
    for sign, rows, far, key, _ in plans:
        if far == 3:
            emit(key + 2, total(y + sign, rows), y + sign)

    for sign, rows, far, key, _ in plans:
        along(key, y).wait_recv()
        value = total(y + sign * (far - 1), rows) + yr[key].astype(F32)
        emit(key + 1, value, y + sign * (far - 1))
    for sign, rows, far, key, _ in plans:
        if far == 4:
            along(key + 2, y).wait_recv()
            value = total(y + sign, rows) + yr[key + 2].astype(F32)
            emit(key + 3, value, y + sign)

    hidden_round(1, 2)
    for index in range(len(HANDED)):
        hidden.handed(index)
    acc[...] = jnp.zeros_like(acc)
    chunk = 4

    @pl.loop(0, 2 * RING // chunk)
    def _(step):
        tokens = pl.ds(step * chunk, chunk)
        left = ga[tokens].reshape(chunk * half, -1)
        right = ha[tokens].reshape(chunk * half, -1)
        acc[...] += lax.dot_general(
            left, right, (((0,), (0,)), ((), ())), preferred_element_type=F32
        )

    def to_sibling(src, dst, key):
        return pltpu.make_async_remote_copy(
            src_ref=src,
            dst_ref=dst,
            send_sem=d_send.at[key],
            recv_sem=d_recv.at[key],
            device_id=sibling,
            device_id_type=MESH,
        )

    weight_swap = to_sibling(acc, acc_in, 0)
    start(weight_swap)
    weight_swap.wait_recv()
    gw_ref[...] = (acc[...] + acc_in[...]).astype(BF16)

    for part in (0, 1):
        rows = pl.ds(part * quarter, quarter)
        value = total(y, rows)
        for sign, _, far, key, which in plans:
            if which == part:
                for last in (key + 1, key + 3 if far == 4 else key + 2):
                    along(last, y).wait_recv()
                    value += yr[last].astype(F32)
        half_s[rows] = value.astype(BF16)
    half_swap = to_sibling(half_s, half_r, 1)
    start(half_swap)
    gh_ref[mine] = half_s[...]
    half_swap.wait_recv()
    gh_ref[pl.ds(pl.multiple_of((1 - depth) * half, half), half)] = half_r[...]
    for copy in sent:
        copy.wait_send()
    @pl.when(lane != grad.lane)
    def _():
        for copy in third:
            copy.wait_send()


def body(grad_out, hidden, weight):
    (tokens, features), units = grad_out.shape, hidden.shape[1]
    half, quarter, blocks = tokens // 2, tokens // 4, 2 * RING
    dma = pltpu.SemaphoreType.DMA
    vmem = pl.BlockSpec(memory_space=pltpu.VMEM)
    grads = len(GRAD_HOPS) + 3
    hiddens = len(HIDDEN_HOPS) + 1 + len(HANDED)
    return pl.pallas_call(
        kernel,
        out_shape=(
            jax.ShapeDtypeStruct(hidden.shape, BF16),
            jax.ShapeDtypeStruct(weight.shape, BF16),
        ),
        in_specs=[vmem] * 3,
        out_specs=(vmem, vmem),
        scratch_shapes=[
            pltpu.VMEM((blocks + RING, half, features), BF16),
            pltpu.VMEM((blocks, half, units), BF16),
            pltpu.VMEM(weight.shape, BF16),
            pltpu.VMEM((RING, half, units), F32),
            pltpu.VMEM((14, quarter, units), BF16),
            pltpu.VMEM((14, quarter, units), BF16),
            pltpu.VMEM((features, units), F32),
            pltpu.VMEM((features, units), F32),
            pltpu.VMEM((half, units), BF16),
            pltpu.VMEM((half, units), BF16),
            dma((grads,)), dma((grads,)), dma((hiddens,)), dma((hiddens,)),
            dma((2,)), dma((2,)), dma((14,)), dma((14,)), dma((2,)), dma((2,)),
        ],
        compiler_params=pltpu.CompilerParams(
            collective_id=0, has_side_effects=True, vmem_limit_bytes=56 << 20
        ),
    )(grad_out, hidden, weight)


def solution(mesh):
    return jax.shard_map(
        body,
        mesh=mesh,
        in_specs=(P("col", "row"), P("row", "col"), P("row", "col")),
        out_specs=(P("row", "col"), P("row", "col")),
        check_vma=False,
    )
```

time: 95.6 us -> 86.3 us (0.903)
  Pallas kernels: 92 us -> 82.7 us
    pallas_call x1, Pallas kernels: 92 us -> 82.7 us  [body(): pl.pallas_call(kernel, out_shape=(jax.ShapeDtypeStruct(hidden.shape, BF16...]
where the time goes in v2:
time: 86.3 us; the launch traced here: 86.2 us
  Pallas kernels  82.7 us (96%)
  local copies, waits for them, and re-layouts  2.83 us (3%)
    pallas_call x1, Pallas kernels, body(): pl.pallas_call(kernel, out_shape=(jax.ShapeDtypeStruct(hidden.shape, BF16...  82.7 us
    unnamed x4, local copies, waits for them, and re-layouts  2.83 us

profile of v2, /device:TPU:1, one launch (start us, length us, event | category | flops | bytes accessed | tf_op | source)
XLA Modules:
  0.0 86.2 jit_solution(17837184234510741466)
XLA Ops:
  0.6 82.7 %shard_map.50 = (bf16[256,896]{1,0:T(8,128)(2,1)}, bf16[512,896]{1,0:T(8,128)(2,1)}) custom-call(bf16[256,512]{1,0:T(8,128)(2,1)} %g_ref.1, bf16[256,896]{1,0:T(8,128)(2,1)} %h_ref.1, bf16[512,896]{1,0:T(8,128)(2,1)} %w_ref.1), custom_call_target="tpu_custom_call" | custom-call | tf_op jit(solution)/shard_map/pallas_call | solution.py:315
  83.3 0.0 copy-start
  83.3 1.9 %copy.7 = bf16[256,896]{1,0:T(8,128)(2,1)} copy(bf16[256,896]{1,0:T(8,128)(2,1)} %get-tuple-element.4) | data formatting | bytes 917504
  85.2 0.0 copy-done
  85.2 0.9 %copy.8 = bf16[512,896]{1,0:T(8,128)(2,1)} copy(bf16[512,896]{1,0:T(8,128)(2,1)S(1)} %copy-done) | data formatting | bytes 1835008
Async XLA Ops:
  83.3 1.9 %copy-start = (bf16[512,896]{1,0:T(8,128)(2,1)S(1)}, bf16[512,896]{1,0:T(8,128)(2,1)}, u32[]{:S(2)}) copy-start(bf16[512,896]{1,0:T(8,128)(2,1)} %get-tuple-element.5) | copy-start | bytes 2752516

commit v3 on v2

--- a/solution.py
+++ b/solution.py
@@ -155,14 +155,6 @@
     for gather in (grad, hidden):
         gather.full[gather.slot(gather.pos, 0)] = gather.own[...]
 
-    def grad_round(hop):
-        for key in GRAD_HOPS:
-            if key[2] == hop:
-                grad.arrived(*key)
-                following = (*key[:2], hop + 1)
-                if following in GRAD_HOPS:
-                    start(grad.hop(*following))
-
     def hidden_round(lane, hop):
         for key in HIDDEN_HOPS:
             if key[1:] == (lane, hop):
@@ -178,47 +170,24 @@
         value = jnp.dot(ga[pos * 2 + lane], w_ref[...], preferred_element_type=F32)
         kept[pos] = value + jnp.dot(ga[2 * RING + pos], wo[...], preferred_element_type=F32)
 
-    def products(hop):
-        product(grad.pos - hop)
-        if hop < 4:
-            product(grad.pos + hop)
-
-    third_arrived()
-    for sign in (1, -1):
-        start(grad.hop(sign, 2, 1))
-    grad.swapped()
-    for sign in (1, -1):
-        start(grad.hop(sign, 1, 1))
-    hidden_round(0, 1)
-    grad_round(1)
-    weights(w_ref, part, 0, partner).wait_recv()
-    start(weights(wo, part, 1, sibling))
-    hidden_round(0, 2)
-    hidden.swapped()
-    for sign in (1, -1):
-        start(hidden.hop(sign, 1, 1))
-    weights(wo, rest, 1, sibling).wait_recv()
-    product(grad.pos)
-    products(1)
-    grad_round(2)
-    hidden_round(0, 3)
-    products(2)
-    hidden_round(1, 1)
-    grad_round(3)
-    products(3)
-    hidden_round(0, 4)
-    grad_round(4)
-    products(4)
-
     def total(pos, rows):
         return kept[wrap(pos), rows]
 
-    plans, at = [], 0
-    for sign in (1, -1):
-        for part in (0, 1):
-            far = 4 if (part == 0) == (sign == 1) else 3
-            plans.append((sign, pl.ds(part * quarter, quarter), far, at, part))
+    plans, singles, sums, at = [], [], [], 0
+    for sign in (1, -1):
+        for piece in (0, 1):
+            far = 4 if (piece == 0) == (sign == 1) else 3
+            rows = pl.ds(piece * quarter, quarter)
+            plans.append((far, at, piece))
+            singles.append((sign * far % RING, at, rows, sign))
+            sums.append((sign * (far - 1) % RING, at, at + 1, rows, sign * (far - 1)))
+            if far == 4:
+                singles.append((sign * 2 % RING, at + 2, rows, sign))
+                sums.append((sign % RING, at + 2, at + 3, rows, sign))
+            else:
+                singles.append((sign % RING, at + 2, rows, sign))
             at += far
+    messages = at
 
     def along(key, pos):
         return pltpu.make_async_remote_copy(
@@ -232,26 +201,77 @@
 
     def emit(key, value, pos):
         ys[key] = value.astype(BF16)
-        start(along(key, pos))
-
-    for sign, rows, far, key, _ in plans:
-        emit(key, total(y + sign * far, rows), y + sign)
-    for sign, rows, far, key, _ in plans:
-        if far == 4:
-            emit(key + 2, total(y + sign * 2, rows), y + sign)
-    for sign, rows, far, key, _ in plans:
-        if far == 3:
-            emit(key + 2, total(y + sign, rows), y + sign)
-
-    for sign, rows, far, key, _ in plans:
-        along(key, y).wait_recv()
-        value = total(y + sign * (far - 1), rows) + yr[key].astype(F32)
-        emit(key + 1, value, y + sign * (far - 1))
-    for sign, rows, far, key, _ in plans:
-        if far == 4:
-            along(key + 2, y).wait_recv()
-            value = total(y + sign, rows) + yr[key + 2].astype(F32)
-            emit(key + 3, value, y + sign)
+        along(key, pos).start()
+
+    def near_and_far(hop):
+        return [grad.pos - hop] + ([grad.pos + hop] if 0 < hop < 4 else [])
+
+    def send_singles(hop):
+        for pos in near_and_far(hop):
+            product(pos)
+            place = lax.rem(wrap(pos) - y + RING, RING)
+            for when in range(1, RING):
+                @pl.when(place == when)
+                def _():
+                    for target, key, rows, to in singles:
+                        if target == when:
+                            emit(key, total(pos, rows), y + to)
+
+    def send_sums(hop):
+        for pos in near_and_far(hop):
+            place = lax.rem(wrap(pos) - y + RING, RING)
+            for when in range(1, RING):
+                @pl.when(place == when)
+                def _():
+                    for target, source, key, rows, to in sums:
+                        if target == when:
+                            along(source, y).wait_recv()
+                            emit(key, total(pos, rows) + yr[source].astype(F32), y + to)
+
+    def grad_lane(lane, hop):
+        for key in GRAD_HOPS:
+            if key[1:] == (lane, hop):
+                grad.arrived(*key)
+                following = (*key[:2], hop + 1)
+                if following in GRAD_HOPS:
+                    start(grad.hop(*following))
+
+    grad_lane(0, 1)
+    third_arrived()
+    for sign in (1, -1):
+        start(grad.hop(sign, 2, 1))
+    grad.swapped()
+    for sign in (1, -1):
+        start(grad.hop(sign, 1, 1))
+    hidden_round(0, 1)
+    weights(w_ref, part, 0, partner).wait_recv()
+    start(weights(wo, part, 1, sibling))
+    hidden_round(0, 2)
+    hidden.swapped()
+    for sign in (1, -1):
+        start(hidden.hop(sign, 1, 1))
+    for which in (1, 2):
+        grad_lane(which, 1)
+    weights(wo, rest, 1, sibling).wait_recv()
+    send_singles(0)
+    send_singles(1)
+    hidden_round(0, 3)
+    for which in (0, 1, 2):
+        grad_lane(which, 2)
+    send_sums(0)
+    send_sums(1)
+    send_singles(2)
+    hidden_round(1, 1)
+    for which in (0, 1, 2):
+        grad_lane(which, 3)
+    send_sums(2)
+    send_singles(3)
+    hidden_round(0, 4)
+    for which in (0, 1, 2):
+        grad_lane(which, 4)
+    send_singles(4)
+    send_sums(3)
+    send_sums(4)
 
     hidden_round(1, 2)
     for index in range(len(HANDED)):
@@ -286,7 +306,7 @@
     for part in (0, 1):
         rows = pl.ds(part * quarter, quarter)
         value = total(y, rows)
-        for sign, _, far, key, which in plans:
+        for far, key, which in plans:
             if which == part:
                 for last in (key + 1, key + 3 if far == 4 else key + 2):
                     along(last, y).wait_recv()
@@ -299,6 +319,8 @@
     gh_ref[pl.ds(pl.multiple_of((1 - depth) * half, half), half)] = half_r[...]
     for copy in sent:
         copy.wait_send()
+    for key in range(messages):
+        along(key, y).wait_send()
     @pl.when(lane != grad.lane)
     def _():
         for copy in third:

time: 86.3 us -> 96.4 us (1.12)
  the two profiles are of different devices: /device:TPU:1 before, /device:TPU:25 now
where the time goes in v3:
time: 96.4 us; the launch traced here: 96.3 us
  Pallas kernels  92.8 us (96%)
  local copies, waits for them, and re-layouts  2.83 us (3%)
    pallas_call x1, Pallas kernels, body(): pl.pallas_call(kernel, out_shape=(jax.ShapeDtypeStruct(hidden.shape, BF16...  92.8 us
    unnamed x4, local copies, waits for them, and re-layouts  2.83 us

profile of v3, /device:TPU:25, one launch (start us, length us, event | category | flops | bytes accessed | tf_op | source)
XLA Modules:
  0.0 96.3 jit_solution(8176798562360479336)
XLA Ops:
  0.6 92.8 %shard_map.50 = (bf16[256,896]{1,0:T(8,128)(2,1)}, bf16[512,896]{1,0:T(8,128)(2,1)}) custom-call(bf16[256,512]{1,0:T(8,128)(2,1)} %g_ref.1, bf16[256,896]{1,0:T(8,128)(2,1)} %h_ref.1, bf16[512,896]{1,0:T(8,128)(2,1)} %w_ref.1), custom_call_target="tpu_custom_call" | custom-call | tf_op jit(solution)/shard_map/pallas_call | solution.py:337
  93.4 0.0 copy-start
  93.4 1.9 %copy.7 = bf16[256,896]{1,0:T(8,128)(2,1)} copy(bf16[256,896]{1,0:T(8,128)(2,1)} %get-tuple-element.4) | data formatting | bytes 917504
  95.3 0.0 copy-done
  95.3 0.9 copy.8
Async XLA Ops:
  93.4 1.9 %copy-start = (bf16[512,896]{1,0:T(8,128)(2,1)S(1)}, bf16[512,896]{1,0:T(8,128)(2,1)}, u32[]{:S(2)}) copy-start(bf16[512,896]{1,0:T(8,128)(2,1)} %get-tuple-element.5) | copy-start | bytes 2752516

commit v4 on v3

--- a/solution.py
+++ b/solution.py
@@ -244,34 +244,33 @@
     for sign in (1, -1):
         start(grad.hop(sign, 1, 1))
     hidden_round(0, 1)
+    grad_lane(0, 2)
+    grad_lane(2, 1)
+    grad_lane(1, 1)
+    hidden_round(0, 2)
+    grad_lane(0, 3)
+    grad_lane(2, 2)
+    grad_lane(1, 2)
     weights(w_ref, part, 0, partner).wait_recv()
     start(weights(wo, part, 1, sibling))
-    hidden_round(0, 2)
-    hidden.swapped()
-    for sign in (1, -1):
-        start(hidden.hop(sign, 1, 1))
-    for which in (1, 2):
-        grad_lane(which, 1)
+    hidden_round(0, 3)
+    grad_lane(2, 3)
+    grad_lane(1, 3)
     weights(wo, rest, 1, sibling).wait_recv()
     send_singles(0)
     send_singles(1)
-    hidden_round(0, 3)
-    for which in (0, 1, 2):
-        grad_lane(which, 2)
-    send_sums(0)
-    send_sums(1)
+    hidden.swapped()
+    for sign in (1, -1):
+        start(hidden.hop(sign, 1, 1))
     send_singles(2)
-    hidden_round(1, 1)
-    for which in (0, 1, 2):
-        grad_lane(which, 3)
-    send_sums(2)
+    hidden_round(0, 4)
     send_singles(3)
-    hidden_round(0, 4)
-    for which in (0, 1, 2):
+    for which in (0, 2, 1):
         grad_lane(which, 4)
     send_singles(4)
-    send_sums(3)
-    send_sums(4)
+    for hop in range(5):
+        send_sums(hop)
+    hidden_round(1, 1)
 
     hidden_round(1, 2)
     for index in range(len(HANDED)):

time: 96.4 us -> 96.9 us (level)
  the two profiles are of different devices: /device:TPU:25 before, /device:TPU:5 now
where the time goes in v4:
time: 96.9 us; the launch traced here: 96.7 us
  Pallas kernels  93.2 us (96%)
  local copies, waits for them, and re-layouts  2.83 us (3%)
    pallas_call x1, Pallas kernels, body(): pl.pallas_call(kernel, out_shape=(jax.ShapeDtypeStruct(hidden.shape, BF16...  93.2 us
    unnamed x4, local copies, waits for them, and re-layouts  2.83 us

profile of v4, /device:TPU:5, one launch (start us, length us, event | category | flops | bytes accessed | tf_op | source)
XLA Modules:
  0.0 96.7 jit_solution(7148292954884050750)
XLA Ops:
  0.6 93.2 %shard_map.50 = (bf16[256,896]{1,0:T(8,128)(2,1)}, bf16[512,896]{1,0:T(8,128)(2,1)}) custom-call(bf16[256,512]{1,0:T(8,128)(2,1)} %g_ref.1, bf16[256,896]{1,0:T(8,128)(2,1)} %h_ref.1, bf16[512,896]{1,0:T(8,128)(2,1)} %w_ref.1), custom_call_target="tpu_custom_call" | custom-call | tf_op jit(solution)/shard_map/pallas_call | solution.py:336
  93.9 0.0 copy-start
  93.9 1.9 %copy.7 = bf16[256,896]{1,0:T(8,128)(2,1)} copy(bf16[256,896]{1,0:T(8,128)(2,1)} %get-tuple-element.4) | data formatting | bytes 917504
  95.8 0.0 copy-done
  95.8 0.9 copy.8
Async XLA Ops:
  93.9 1.9 %copy-start = (bf16[512,896]{1,0:T(8,128)(2,1)S(1)}, bf16[512,896]{1,0:T(8,128)(2,1)}, u32[]{:S(2)}) copy-start(bf16[512,896]{1,0:T(8,128)(2,1)} %get-tuple-element.5) | copy-start | bytes 2752516

commit v5 on v4

--- a/solution.py
+++ b/solution.py
@@ -13,11 +13,12 @@
     for hop in (1, 2, 3, 4)
     for lane in (0, 1, 2)
     for sign in (1, -1)
-    if hop < 4 or (sign == 1) == (lane != 1)
+    if ((sign, hop) in ((1, 1), (-1, 1), (-1, 2)) if lane == 2 else hop < 4 or (sign == 1) == (lane == 0))
 ]
+THIRDS = [(1, 0, 2), (1, 0, 3), (-1, 0, 3), (1, 0, 4)]
 HIDDEN_HOPS = [(1, 0, 1), (-1, 0, 1), (1, 0, 2), (-1, 0, 2), (1, 0, 3), (-1, 0, 3), (1, 0, 4)]
-HIDDEN_HOPS += [(1, 1, 1), (-1, 1, 1), (-1, 1, 2)]
-HANDED = [(1, 0, 2), (1, 0, 3), (-1, 0, 3), (1, 0, 4)]
+HIDDEN_HOPS += [(1, 1, 1), (-1, 1, 1), (1, 1, 2), (-1, 1, 2)]
+HANDED = [(1, 0, 3), (-1, 0, 3), (1, 0, 4)]
 
 
 def wrap(pos):
@@ -118,14 +119,29 @@
         sent.append(copy)
 
     lane_2 = len(GRAD_HOPS) + 1
-    third = [grad.copy(grad.own, grad.slot(grad.pos, 2), lane_2 + i, to) for i, to in enumerate((partner, across))]
-
-    def third_arrived():
-        slot = grad.slot(grad.pos, 2)
-        for i, (source, here) in enumerate(((partner, lane == grad.lane), (across, lane != grad.lane))):
-            @pl.when(here)
-            def _():
-                grad.copy(ga.at[slot], slot, lane_2 + i, source).wait_recv()
+    def thirds(index):
+        if index == len(THIRDS):
+            pos, src = grad.pos, grad.own
+        else:
+            sign, _, hop = THIRDS[index]
+            pos = grad.pos - sign * hop
+            src = ga.at[grad.slot(pos, 0)]
+        slot, key = grad.slot(pos, 2), lane_2 + 2 * index
+        return [grad.copy(src, slot, key + i, to) for i, to in enumerate((partner, across))]
+
+    def send_thirds(index):
+        @pl.when(lane != grad.lane)
+        def _():
+            for copy in thirds(index):
+                copy.start()
+
+    def third_arrived(index):
+        @pl.when(lane == grad.lane)
+        def _():
+            thirds(index)[0].wait_recv()
+        @pl.when(lane != grad.lane)
+        def _():
+            thirds(index)[1].wait_recv()
 
     features = w_ref.shape[0] // 2
     part = pl.ds(pl.multiple_of(depth * features, features), features)
@@ -143,10 +159,7 @@
 
     for sign in (1, -1):
         start(grad.hop(sign, 0, 1))
-    @pl.when(lane != grad.lane)
-    def _():
-        for copy in third:
-            copy.start()
+    send_thirds(len(THIRDS))
     start(grad.swap())
     for sign in (1, -1):
         start(hidden.hop(sign, 0, 1))
@@ -162,8 +175,6 @@
                 following = (*key[:2], hop + 1)
                 if following in HIDDEN_HOPS:
                     start(hidden.hop(*following))
-                if key in HANDED:
-                    start(hidden.hand(HANDED.index(key)))
 
     def product(pos):
         pos = wrap(pos)
@@ -235,43 +246,65 @@
                 following = (*key[:2], hop + 1)
                 if following in GRAD_HOPS:
                     start(grad.hop(*following))
+                if key in THIRDS:
+                    send_thirds(THIRDS.index(key))
 
     grad_lane(0, 1)
-    third_arrived()
+    third_arrived(len(THIRDS))
     for sign in (1, -1):
         start(grad.hop(sign, 2, 1))
     grad.swapped()
     for sign in (1, -1):
         start(grad.hop(sign, 1, 1))
     hidden_round(0, 1)
-    grad_lane(0, 2)
     grad_lane(2, 1)
     grad_lane(1, 1)
+    weights(w_ref, part, 0, partner).wait_recv()
+    start(weights(wo, part, 1, sibling))
+    grad_lane(0, 2)
     hidden_round(0, 2)
-    grad_lane(0, 3)
+    weights(wo, rest, 1, sibling).wait_recv()
+    for hop in (0,):
+        for pos in near_and_far(hop):
+            product(pos)
     grad_lane(2, 2)
     grad_lane(1, 2)
-    weights(w_ref, part, 0, partner).wait_recv()
-    start(weights(wo, part, 1, sibling))
+    for hop in (1,):
+        for pos in near_and_far(hop):
+            product(pos)
+    grad_lane(0, 3)
+    hidden.swapped()
+    for sign in (1, -1):
+        start(hidden.hop(sign, 1, 1))
     hidden_round(0, 3)
+    third_arrived(0)
+    for hop in (2,):
+        for pos in near_and_far(hop):
+            product(pos)
     grad_lane(2, 3)
     grad_lane(1, 3)
-    weights(wo, rest, 1, sibling).wait_recv()
-    send_singles(0)
-    send_singles(1)
-    hidden.swapped()
-    for sign in (1, -1):
-        start(hidden.hop(sign, 1, 1))
-    send_singles(2)
     hidden_round(0, 4)
-    send_singles(3)
-    for which in (0, 2, 1):
+    third_arrived(1)
+    third_arrived(2)
+    for index in (0, 1):
+        start(hidden.hand(index))
+    for hop in (3,):
+        for pos in near_and_far(hop):
+            product(pos)
+    hidden_round(1, 1)
+    for which in (0, 1):
         grad_lane(which, 4)
-    send_singles(4)
-    for hop in range(5):
-        send_sums(hop)
-    hidden_round(1, 1)
-
+    start(hidden.hand(2))
+    third_arrived(3)
+    for hop in (4,):
+        for pos in near_and_far(hop):
+            product(pos)
+    heads = [key for far, key, _ in plans]
+    for _, key, rows, to in sorted(singles, key=lambda m: m[1] not in heads):
+        emit(key, total(y + _ , rows), y + to)
+    for _, source, key, rows, to in sorted(sums, key=lambda m: m[1] not in heads):
+        along(source, y).wait_recv()
+        emit(key, total(y + _, rows) + yr[source].astype(F32), y + to)
     hidden_round(1, 2)
     for index in range(len(HANDED)):
         hidden.handed(index)
@@ -322,8 +355,9 @@
         along(key, y).wait_send()
     @pl.when(lane != grad.lane)
     def _():
-        for copy in third:
-            copy.wait_send()
+        for index in range(len(THIRDS) + 1):
+            for copy in thirds(index):
+                copy.wait_send()
 
 
 def body(grad_out, hidden, weight):
@@ -331,7 +365,7 @@
     half, quarter, blocks = tokens // 2, tokens // 4, 2 * RING
     dma = pltpu.SemaphoreType.DMA
     vmem = pl.BlockSpec(memory_space=pltpu.VMEM)
-    grads = len(GRAD_HOPS) + 3
+    grads = len(GRAD_HOPS) + 3 + 2 * len(THIRDS)
     hiddens = len(HIDDEN_HOPS) + 1 + len(HANDED)
     return pl.pallas_call(
         kernel,

time: 96.9 us -> 93.7 us (0.967)
  the two profiles are of different devices: /device:TPU:5 before, /device:TPU:1 now
where the time goes in v5:
time: 93.7 us; the launch traced here: 93.6 us
  Pallas kernels  90.1 us (96%)
  local copies, waits for them, and re-layouts  2.83 us (3%)
    pallas_call x1, Pallas kernels, body(): pl.pallas_call(kernel, out_shape=(jax.ShapeDtypeStruct(hidden.shape, BF16...  90.1 us
    unnamed x4, local copies, waits for them, and re-layouts  2.83 us

profile of v5, /device:TPU:1, one launch (start us, length us, event | category | flops | bytes accessed | tf_op | source)
XLA Modules:
  0.0 93.6 jit_solution(16812996329922077494)
XLA Ops:
  0.6 90.1 %shard_map.50 = (bf16[256,896]{1,0:T(8,128)(2,1)}, bf16[512,896]{1,0:T(8,128)(2,1)}) custom-call(bf16[256,512]{1,0:T(8,128)(2,1)} %g_ref.1, bf16[256,896]{1,0:T(8,128)(2,1)} %h_ref.1, bf16[512,896]{1,0:T(8,128)(2,1)} %w_ref.1), custom_call_target="tpu_custom_call" | custom-call | tf_op jit(solution)/shard_map/pallas_call | solution.py:370
  90.7 0.0 copy-start
  90.7 1.9 %copy.7 = bf16[256,896]{1,0:T(8,128)(2,1)} copy(bf16[256,896]{1,0:T(8,128)(2,1)} %get-tuple-element.4) | data formatting | bytes 917504
  92.7 0.0 copy-done
  92.7 0.9 copy.8
Async XLA Ops:
  90.7 1.9 %copy-start = (bf16[512,896]{1,0:T(8,128)(2,1)S(1)}, bf16[512,896]{1,0:T(8,128)(2,1)}, u32[]{:S(2)}) copy-start(bf16[512,896]{1,0:T(8,128)(2,1)} %get-tuple-element.5) | copy-start | bytes 2752516

commit v6 on v4

--- a/solution.py
+++ b/solution.py
@@ -150,8 +150,6 @@
     start(grad.swap())
     for sign in (1, -1):
         start(hidden.hop(sign, 0, 1))
-    start(weights(w_ref, part, 0, partner))
-    start(hidden.swap())
     for gather in (grad, hidden):
         gather.full[gather.slot(gather.pos, 0)] = gather.own[...]
 
@@ -241,36 +239,59 @@
     for sign in (1, -1):
         start(grad.hop(sign, 2, 1))
     grad.swapped()
+    start(weights(w_ref, part, 0, partner))
     for sign in (1, -1):
         start(grad.hop(sign, 1, 1))
     hidden_round(0, 1)
-    grad_lane(0, 2)
     grad_lane(2, 1)
     grad_lane(1, 1)
+    weights(w_ref, part, 0, partner).wait_recv()
+    start(weights(wo, part, 1, sibling))
+    start(hidden.swap())
+    grad_lane(0, 2)
     hidden_round(0, 2)
-    grad_lane(0, 3)
+    weights(wo, rest, 1, sibling).wait_recv()
+    for hop in (0,):
+        for pos in near_and_far(hop):
+            product(pos)
     grad_lane(2, 2)
     grad_lane(1, 2)
-    weights(w_ref, part, 0, partner).wait_recv()
-    start(weights(wo, part, 1, sibling))
+    for hop in (1,):
+        for pos in near_and_far(hop):
+            product(pos)
+    grad_lane(0, 3)
+    hidden.swapped()
+    for sign in (1, -1):
+        start(hidden.hop(sign, 1, 1))
     hidden_round(0, 3)
+    for hop in (2,):
+        for pos in near_and_far(hop):
+            product(pos)
     grad_lane(2, 3)
     grad_lane(1, 3)
-    weights(wo, rest, 1, sibling).wait_recv()
-    send_singles(0)
-    send_singles(1)
-    hidden.swapped()
-    for sign in (1, -1):
-        start(hidden.hop(sign, 1, 1))
-    send_singles(2)
     hidden_round(0, 4)
-    send_singles(3)
+    for hop in (3,):
+        for pos in near_and_far(hop):
+            product(pos)
+    hidden_round(1, 1)
     for which in (0, 2, 1):
         grad_lane(which, 4)
-    send_singles(4)
-    for hop in range(5):
-        send_sums(hop)
-    hidden_round(1, 1)
+    for hop in (4,):
+        for pos in near_and_far(hop):
+            product(pos)
+    chains, at = [], 0
+    for far, _, piece in plans:
+        sign = 1 if (piece == 0) == (far == 4) else -1
+        chains.append((sign, pl.ds(piece * quarter, quarter), far, at))
+        at += far
+    for step in range(4):
+        for sign, rows, far, key in chains:
+            if step < far:
+                value = total(y + sign * (far - step), rows)
+                if step:
+                    along(key + step - 1, y).wait_recv()
+                    value += yr[key + step - 1].astype(F32)
+                emit(key + step, value, y + sign)
 
     hidden_round(1, 2)
     for index in range(len(HANDED)):
@@ -307,7 +328,7 @@
         value = total(y, rows)
         for far, key, which in plans:
             if which == part:
-                for last in (key + 1, key + 3 if far == 4 else key + 2):
+                for last in (key + far - 1,):
                     along(last, y).wait_recv()
                     value += yr[last].astype(F32)
         half_s[rows] = value.astype(BF16)

time: 96.9 us -> 83.7 us (0.86)
  the two profiles are of different devices: /device:TPU:5 before, /device:TPU:1 now
where the time goes in v6:
time: 83.7 us; the launch traced here: 83.5 us
  Pallas kernels  80 us (96%)
  local copies, waits for them, and re-layouts  2.83 us (3%)
    pallas_call x1, Pallas kernels, body(): pl.pallas_call(kernel, out_shape=(jax.ShapeDtypeStruct(hidden.shape, BF16...  80 us
    unnamed x4, local copies, waits for them, and re-layouts  2.83 us

profile of v6, /device:TPU:1, one launch (start us, length us, event | category | flops | bytes accessed | tf_op | source)
XLA Modules:
  0.0 83.5 jit_solution(3752106815567939704)
XLA Ops:
  0.6 80.0 %shard_map.50 = (bf16[256,896]{1,0:T(8,128)(2,1)}, bf16[512,896]{1,0:T(8,128)(2,1)}) custom-call(bf16[256,512]{1,0:T(8,128)(2,1)} %g_ref.1, bf16[256,896]{1,0:T(8,128)(2,1)} %h_ref.1, bf16[512,896]{1,0:T(8,128)(2,1)} %w_ref.1), custom_call_target="tpu_custom_call" | custom-call | tf_op jit(solution)/shard_map/pallas_call | solution.py:357
  80.6 0.0 copy-start
  80.7 1.9 %copy.7 = bf16[256,896]{1,0:T(8,128)(2,1)} copy(bf16[256,896]{1,0:T(8,128)(2,1)} %get-tuple-element.4) | data formatting | bytes 917504
  82.6 0.0 copy-done
  82.6 0.9 %copy.8 = bf16[512,896]{1,0:T(8,128)(2,1)} copy(bf16[512,896]{1,0:T(8,128)(2,1)S(1)} %copy-done) | data formatting | bytes 1835008
Async XLA Ops:
  80.6 1.9 %copy-start = (bf16[512,896]{1,0:T(8,128)(2,1)S(1)}, bf16[512,896]{1,0:T(8,128)(2,1)}, u32[]{:S(2)}) copy-start(bf16[512,896]{1,0:T(8,128)(2,1)} %get-tuple-element.5) | copy-start | bytes 2752516
